TPU v7x, 128 devices: a whole 4x4x4 slice. The times are simulated.
128 devices in a mesh: gx: 8 (over x_hi, z), gy: 16 (over y, x_lo, core).
Axes of the slice: x: 4 (x_hi: 2, x_lo: 2; x = x_hi * 2 + x_lo), y: 4, z: 4, core: 2. Of those that a mesh axis runs over, the one named last changes fastest.
Arguments:
- fine_state: float32 [9, 16, 512, 2048], P(None, None, 'gx', 'gy'), may hold values from -6 to 6
- fine_medium: float32 [3, 16, 512, 2048], P(None, None, 'gx', 'gy'), may hold values from 0.5 to 2
- coarse_state: float32 [9, 8, 256, 1024], P(None, None, 'gy', 'gx'), may hold values from -6 to 6
- coarse_medium: float32 [3, 8, 256, 1024], P(None, None, 'gy', 'gx'), may hold values from 0.5 to 2
- coarse_past: float32 [9, 2, 256, 1024], P(None, None, 'gy', 'gx'), may hold values from -6 to 6
- parent_rows: int32 [512], P('gx'), may hold values from 0 to 255, as said below
- parent_cols: int32 [2048], P('gy'), may hold values from 0 to 1023, as said below
Outputs:
- fine_out: float32 [9, 16, 512, 2048], P(None, None, 'gx', 'gy')
- coarse_out: float32 [9, 8, 256, 1024], P(None, None, 'gy', 'gx')
Inputs may be any that keep to these rules, and one draw needn't show every extreme that they name: parent_rows[x] is x / 2 - 1 for x a positive multiple of 4, 0 for x = 0, x / 2 for x of remainder 2 by 4, (x - 1) / 2 or (x + 1) / 2 for remainder 1, and (x + 1) / 2 for remainder 3, never past the last coarse row. parent_cols[y] follows the same rule along columns, never past the last coarse column.
All inputs are finite; a program needn't handle non-finite values.
Results may differ from a plain program's by a relative error of at most 0.00002.
Values sent between devices are 32-bit elements; how exact they have to be, the bound alone decides.
A program may use at most 192 MiB of HBM per device.

v0:
```python
import jax
import jax.numpy as jnp
from jax import lax
from jax.sharding import PartitionSpec as P

COEFFS = (1225.0 / 1024.0, -245.0 / 3072.0, 49.0 / 5120.0, -5.0 / 7168.0)
STEP = 0.1


def extended(x, sides, width):
    for axis, dim in sides:
        peers, length = (lax.axis_size(axis), x.shape[dim])
        up = [(i, (i + 1) % peers) for i in range(peers - 1)]
        down = [(j, i) for i, j in up]
        last = lax.slice_in_dim(x, length - width, length, axis=dim)
        leading = lax.slice_in_dim(x, 0, width, axis=dim)
        before = lax.ppermute(last, axis, up)
        after = lax.ppermute(leading, axis, down)
        x = jnp.concatenate([before, x, after], axis=dim)
    return x


def derivative(values, dimension, forward, inv_spacing):
    rank_count = values.ndim
    dimension = dimension % rank_count
    cropped = values
    for other_dim in range(rank_count - 3, rank_count):
        if other_dim != dimension:
            cropped = lax.slice_in_dim(cropped, 4, cropped.shape[other_dim] - 4, axis=other_dim)
    length = cropped.shape[dimension] - 8
    result = None
    for tap_index in range(1, 5):
        upper_start = 4 + tap_index if forward else 3 + tap_index
        lower_start = 5 - tap_index if forward else 4 - tap_index
        upper_part = lax.slice_in_dim(cropped, upper_start, upper_start + length, axis=dimension)
        lower_part = lax.slice_in_dim(cropped, lower_start, lower_start + length, axis=dimension)
        tap_term = COEFFS[tap_index - 1] * (upper_part - lower_part)
        result = tap_term if result is None else result + tap_term
    return result * inv_spacing


def velocity_step(velocity, stress_pad, buoyancy, step_size, inv_spacing):
    first_rate = (
        derivative(stress_pad[0], -2, True, inv_spacing)
        + derivative(stress_pad[3], -1, False, inv_spacing)
        + derivative(stress_pad[4], -3, False, inv_spacing)
    )
    second_rate = (
        derivative(stress_pad[3], -2, False, inv_spacing)
        + derivative(stress_pad[1], -1, True, inv_spacing)
        + derivative(stress_pad[5], -3, False, inv_spacing)
    )
    third_rate = (
        derivative(stress_pad[4], -2, False, inv_spacing)
        + derivative(stress_pad[5], -1, False, inv_spacing)
        + derivative(stress_pad[2], -3, True, inv_spacing)
    )
    return velocity + step_size * buoyancy * jnp.stack([first_rate, second_rate, third_rate])


def stress_step(stress, velocity_pad, lame_first, shear_modulus, step_size, inv_spacing):
    strain_first = derivative(velocity_pad[0], -2, False, inv_spacing)
    strain_second = derivative(velocity_pad[1], -1, False, inv_spacing)
    strain_third = derivative(velocity_pad[2], -3, False, inv_spacing)
    dilation = strain_first + strain_second + strain_third
    rate_list = [
        lame_first * dilation + 2.0 * shear_modulus * strain_first,
        lame_first * dilation + 2.0 * shear_modulus * strain_second,
        lame_first * dilation + 2.0 * shear_modulus * strain_third,
        shear_modulus
        * (
            derivative(velocity_pad[0], -1, True, inv_spacing)
            + derivative(velocity_pad[1], -2, True, inv_spacing)
        ),
        shear_modulus
        * (
            derivative(velocity_pad[0], -3, True, inv_spacing)
            + derivative(velocity_pad[2], -2, True, inv_spacing)
        ),
        shear_modulus
        * (
            derivative(velocity_pad[1], -3, True, inv_spacing)
            + derivative(velocity_pad[2], -1, True, inv_spacing)
        ),
    ]
    return stress + step_size * jnp.stack(rate_list)


def zero_layers(values, layer_count):
    return jnp.zeros((values.shape[0], layer_count) + values.shape[2:], values.dtype)


def widen_ghost(widened, ghost_cells):
    margin = (widened.shape[-1] - ghost_cells.shape[-1]) // 2
    return jnp.pad(ghost_cells, ((0, 0), (0, 0), (margin, margin), (margin, margin)))


def below_pad(widened, ghost_cells):
    return jnp.concatenate(
        [zero_layers(widened, 4), widened, widen_ghost(widened, ghost_cells)], axis=1
    )


def above_pad(widened, ghost_cells):
    return jnp.concatenate(
        [widen_ghost(widened, ghost_cells), widened, zero_layers(widened, 4)], axis=1
    )


def fine_rim(values):
    return extended(values, (("gx", 2), ("gy", 3)), 4)


def coarse_rim(values):
    return extended(values, (("gx", 3), ("gy", 2)), 4)


def regrid(planes):
    devices_x = lax.axis_size("gx")
    ratio_xy = lax.axis_size("gy") // devices_x
    lead_count, rows_in, cols_in = planes.shape
    piece_cols = cols_in // ratio_xy // devices_x
    sectioned = planes.reshape(lead_count, 1, rows_in, ratio_xy, devices_x, piece_cols)
    moved_pair = lax.all_to_all(
        lax.all_to_all(sectioned, "gx", split_axis=4, concat_axis=3, tiled=True),
        "gy",
        split_axis=3,
        concat_axis=1,
        tiled=True,
    )
    settled = lax.all_to_all(moved_pair, "gx", split_axis=1, concat_axis=4, tiled=True)
    return settled.reshape(lead_count, ratio_xy * rows_in, cols_in // ratio_xy)


def body(
    fine_state, fine_medium, coarse_state, coarse_medium, coarse_past, parent_rows, parent_cols
):
    fine_depth = fine_state.shape[1]
    rows_half = fine_state.shape[2] // 2
    cols_half = fine_state.shape[3] // 2
    coarse_top = coarse_state[:, :2]
    plane_rows = coarse_top.shape[2]
    plane_cols = coarse_top.shape[3]
    moved_top = regrid(coarse_top.reshape(-1, plane_rows, plane_cols))
    moved_past = regrid(coarse_past.reshape(-1, plane_rows, plane_cols))
    moved_planes = jnp.concatenate([moved_top, 1.5 * moved_top - 0.5 * moved_past], axis=0)
    widened = extended(moved_planes, (("gx", 1), ("gy", 2)), 1)
    local_rows = parent_rows - lax.axis_index("gx") * rows_half + 1
    local_cols = parent_cols - lax.axis_index("gy") * cols_half + 1
    picked = jnp.take(jnp.take(widened, local_rows, axis=1), local_cols, axis=2)
    picked = picked.reshape((2, 9, 2) + picked.shape[1:])
    ghosts = jnp.repeat(picked, 2, axis=2)
    lame_first = fine_medium[1]
    shear_modulus = fine_medium[2]
    fine_now = fine_state
    for level_index in range(2):
        ghost_cells = ghosts[level_index]
        stress_pad = below_pad(fine_rim(fine_now[3:]), ghost_cells[3:])
        velocity = velocity_step(fine_now[:3], stress_pad, fine_medium[0], STEP, 1.0)
        velocity_pad = below_pad(fine_rim(velocity), ghost_cells[:3])
        stress = stress_step(fine_now[3:], velocity_pad, lame_first, shear_modulus, STEP, 1.0)
        fine_now = jnp.concatenate([velocity, stress], axis=0)
    blended = 0.5 * (fine_state[:, fine_depth - 8 :] + fine_now[:, fine_depth - 8 :])
    restricted = blended.reshape(9, 4, 2, rows_half, 2, cols_half, 2).mean(axis=(2, 4, 6))
    flipped = jnp.swapaxes(restricted, 2, 3).reshape(36, cols_half, rows_half)
    lifted = regrid(flipped)
    coarse_ghost = jnp.swapaxes(lifted.reshape(9, 4, lifted.shape[1], lifted.shape[2]), 2, 3)
    stress_pad = above_pad(coarse_rim(coarse_state[3:]), coarse_ghost[3:])
    velocity = velocity_step(coarse_state[:3], stress_pad, coarse_medium[0], 2.0 * STEP, 0.5)
    velocity_pad = above_pad(coarse_rim(velocity), coarse_ghost[:3])
    stress = stress_step(
        coarse_state[3:], velocity_pad, coarse_medium[1], coarse_medium[2], 2.0 * STEP, 0.5
    )
    coarse_out = jnp.concatenate([velocity, stress], axis=0)
    return (fine_now, coarse_out)


def solution(mesh):
    placed = (
        P(None, None, "gx", "gy"),
        P(None, None, "gx", "gy"),
        P(None, None, "gy", "gx"),
        P(None, None, "gy", "gx"),
        P(None, None, "gy", "gx"),
        P("gx"),
        P("gy"),
    )
    return jax.shard_map(
        body,
        mesh=mesh,
        in_specs=placed,
        out_specs=(P(None, None, "gx", "gy"), P(None, None, "gy", "gx")),
        check_vma=False,
    )
```

profile of v0, /device:TPU:28, one launch (start us, length us, event | category | flops | bytes accessed | tf_op | source)
XLA Modules:
  0.0 675.0 jit_solution(6099651927591401546)
XLA Ops:
  4.6 8.3 %all-to-all-start.3 = ((f32[8,1,4608]{2,1,0:T(1,128)}), f32[8,1,4608]{2,1,0:T(1,128)S(1)}, u32[]{:S(2)}, u32[]{:S(2)}) async-start(f32[8,1,4608]{2,1,0:T(1,128)} %reshape.93), calls=%async_computation.3 | async-start | bytes 294912 | tf_op jit(solution)/shard_map/all_to_all | solution.py:125
  28.2 7.5 %all-to-all-start = ((f32[8,1,4608]{2,1,0:T(1,128)}), f32[8,1,4608]{2,1,0:T(1,128)S(1)}, u32[]{:S(2)}, u32[]{:S(2)}) async-start(f32[8,1,4608]{2,1,0:T(1,128)} %reshape.99), calls=%async_computation | async-start | bytes 294912 | tf_op jit(solution)/shard_map/all_to_all | solution.py:125
  80.3 6.6 all-to-all-start.1
  103.1 6.7 all-to-all-start.2
  127.4 6.5 maximum_bitcast_fusion.7
  178.8 9.8 %select_maximum_fusion.1 = f32[6,24,72,136]{2,1,3,0:T(8,128)S(1)} fusion(f32[6,4,64,128]{2,1,3,0:T(4,128)S(1)} %bitcast.334, f32[6,16,72,4]{2,1,3,0:T(8,128)S(1)} %collective-permute-done.3, f32[6,16,4,128]{2,1,3,0:T(8,128)} %copy.146, f32[6,16,64,128]{2,1,3,0:T(8,128)} %copy.200, f32[6,16,4,128]{2,1,3,0:T(8,128)} %copy.145, ...), kind=kLoop, calls=%fused_computation.6 | loop fusion | flops 11280384 | bytes 10186848 | tf_op jit(solution)/shard_map/concatenate | solution.py:99
  189.9 6.4 fusion.258
  196.2 6.6 fusion.282
  202.9 6.6 fusion.234
  215.9 6.8 %collective-permute-start.9 = (f32[3,16,4,128]{3,1,2,0:T(8,128)S(1)}, f32[3,16,4,128]{3,1,2,0:T(8,128)S(1)}, u32[]{:S(2)}, u32[]{:S(2)}) collective-permute-start(f32[3,16,4,128]{3,1,2,0:T(8,128)S(1)} %copy.173), channel_id=1, source_target_pairs={{16,0},{32,16},{48,32},{64,48},{80,64},{96,80},{112,96},{17,1},{33... | collective-permute-start | bytes 294920 | tf_op jit(solution)/shard_map/ppermute | solution.py:18
  261.7 7.3 %bitcast_dynamic-update-slice_fusion.5 = (f32[6,16,64,128]{2,1,3,0:T(8,128)}, f32[16,64,128]{1,0,2:T(8,128)S(1)}, f32[16,64,128]{1,0,2:T(8,128)S(1)}, f32[16,64,128]{1,0,2:T(8,128)S(1)}) fusion(f32[1,16,64,128]{2,1,3,0:T(8,128)S(1)} %copy.203, f32[1,16,64,128]{2,1,3,0:T(8,128)S(1)} %copy.202, f32[16,72,136]{1,0,2:T(8,128)S(1)} %get-tuple-element.62, ...), kind=kLoop, calls=%fused_computation.509 | loop fusion | flops 5111807 | bytes 16252928
  291.4 6.8 %fusion.467 = (f32[6,16,4,128]{2,1,3,0:T(8,128)}, f32[6,16,4,128]{2,1,3,0:T(8,128)}) fusion(f32[6,16,64,128]{2,1,3,0:T(8,128)S(1)} %multiply_add_fusion.1), kind=kLoop, calls=%fused_computation.806 | loop fusion | bytes 786432 | tf_op jit(solution)/shard_map/slice | solution.py:15
  341.8 15.1 %select_maximum_fusion = f32[6,24,72,136]{2,1,3,0:T(8,128)} fusion(f32[6,4,64,128]{2,1,3,0:T(4,128)S(1)} %bitcast.335, f32[6,16,72,4]{2,1,3,0:T(8,128)S(1)} %collective-permute-done.15, f32[6,16,4,128]{2,1,3,0:T(8,128)} %copy.181, f32[6,16,64,128]{2,1,3,0:T(8,128)} %copy-done, f32[6,16,4,128]{2,1,3,0:T(8,128)} %copy.180, ...), kind=kLoop, calls=%fused_computation.5 | loop fusion | flops 11280384 | bytes 10186848 | tf_op jit(solution)/shard_map/concatenate | solution.py:99
  366.3 11.7 %fusion.111 = f32[1,16,64,128]{2,1,3,0:T(8,128)S(1)} fusion(f32[24,72,136]{1,0,2:T(8,128)} %get-tuple-element.40, f32[16,72,136]{1,0,2:T(8,128)S(1)} %get-tuple-element.26, f32[16,72,136]{1,0,2:T(8,128)S(1)} %get-tuple-element.27), kind=kLoop, calls=%fused_computation.217 | loop fusion | flops 4587520 | bytes 13107200 | tf_op jit(solution)/shard_map/stack | solution.py:58
  378.1 7.1 %fusion.135 = f32[1,16,64,128]{2,1,3,0:T(8,128)S(1)} fusion(f32[24,72,136]{1,0,2:T(8,128)S(1)} %copy-done.9, f32[16,72,136]{1,0,2:T(8,128)S(1)} %get-tuple-element.27, f32[16,72,136]{1,0,2:T(8,128)S(1)} %get-tuple-element.24), kind=kLoop, calls=%fused_computation.253 | loop fusion | flops 4587520 | bytes 13107200 | tf_op jit(solution)/shard_map/stack | solution.py:58
  385.2 6.4 fusion.87
  445.9 7.2 %bitcast_dynamic-update-slice_fusion.2 = (f32[6,16,64,128]{2,1,3,0:T(8,128)}, f32[16,64,128]{1,0,2:T(8,128)S(1)}, f32[16,64,128]{1,0,2:T(8,128)S(1)}, f32[16,64,128]{1,0,2:T(8,128)S(1)}) fusion(f32[1,16,64,128]{2,1,3,0:T(8,128)S(1)} %copy-done.2, f32[1,16,64,128]{2,1,3,0:T(8,128)S(1)} %copy-done.18, f32[16,72,136]{1,0,2:T(8,128)S(1)} %get-tuple-element.59, ...), kind=kLoop, calls=%fused_computation.506 | loop fusion | flops 5111807 | bytes 16252928
  483.2 19.2 %copy.189 = f32[9,8,64,128]{0,3,2,1:T(8,128)} copy(f32[9,8,64,128]{2,1,3,0:T(8,128)} %fusion.2) | data formatting | bytes 4718592 | tf_op jit(solution)/shard_map/mul | solution.py:163
  502.4 24.3 %reduce_sum.9 = f32[9,4,32,64]{0,3,2,1:T(8,128)} reduce(f32[9,4,2,32,2,64,2]{0,6,5,4,3,2,1:T(2,128)} %bitcast.333, f32[]{:T(128)} %constant.28.clone.1), dimensions={2,4,6}, to_apply=%region_0.1 | reduce | flops 516096 | bytes 2654212 | tf_op jit(solution)/shard_map/reduce_sum | solution.py:164
  539.2 11.7 %all_to_all.147 = f32[8,1,9216]{2,1,0:T(1,128)} all-to-all(f32[8,1,9216]{2,1,0:T(1,128)S(1)} %reshape.105), channel_id=1, replica_groups=mesh['gx'=8,'gy'=16] {'gx'}, dimensions={0} | all-to-all | bytes 589824 | tf_op jit(solution)/shard_map/all_to_all | solution.py:125
  579.5 7.7 %collective-permute-done.20 = f32[6,8,16,4]{3,2,1,0:T(8,128)S(1)} collective-permute-done((f32[6,8,16,4]{3,2,1,0:T(8,128)S(1)}, f32[6,8,16,4]{3,2,1,0:T(8,128)S(1)}, u32[]{:S(2)}, u32[]{:S(2)}) %collective-permute-start.20) | collective-permute-done | bytes 12320 | tf_op jit(solution)/shard_map/ppermute | solution.py:17
  638.8 7.7 %collective-permute-done.24 = f32[3,8,16,4]{3,2,1,0:T(8,128)S(1)} collective-permute-done((f32[3,8,16,4]{3,2,1,0:T(8,128)S(1)}, f32[3,8,16,4]{3,2,1,0:T(8,128)S(1)}, u32[]{:S(2)}, u32[]{:S(2)}) %collective-permute-start.24) | collective-permute-done | bytes 6176 | tf_op jit(solution)/shard_map/ppermute | solution.py:17
  652.6 7.4 %pad_maximum_fusion = f32[9,16,64,128]{2,1,3,0:T(8,128)} fusion(f32[3,16,64,128]{2,1,3,0:T(8,128)S(1)} %fusion.4, f32[6,16,64,128]{2,1,3,0:T(8,128)} %copy-done.10), kind=kLoop, calls=%fused_computation.3 | loop fusion | flops 1179648 | bytes 9437184 | tf_op jit(solution)/shard_map/concatenate | solution.py:162
  660.0 8.6 %copy.197 = f32[9,16,64,128]{3,2,1,0:T(8,128)} copy(f32[9,16,64,128]{2,1,3,0:T(8,128)} %pad_maximum_fusion) | data formatting | bytes 9437184
  (374 shorter events, 452.5 us)
Async XLA Ops:
  4.6 23.6 %all-to-all-start.3 = ((f32[8,1,4608]{2,1,0:T(1,128)}), f32[8,1,4608]{2,1,0:T(1,128)S(1)}, u32[]{:S(2)}, u32[]{:S(2)}) async-start(f32[8,1,4608]{2,1,0:T(1,128)} %reshape.93), calls=%async_computation.3 | async-start | bytes 294912 | tf_op jit(solution)/shard_map/all_to_all | solution.py:125
  14.8 47.7 %collective-permute-start.1 = (f32[6,16,4,128]{3,1,2,0:T(8,128)}, f32[6,16,4,128]{3,1,2,0:T(8,128)}, u32[]{:S(2)}, u32[]{:S(2)}) collective-permute-start(f32[6,16,4,128]{3,1,2,0:T(8,128)} %copy.201), channel_id=1, source_target_pairs={{16,0},{32,16},{48,32},{64,48},{80,64},{96,80},{112,96},{17,1},{33... | collective-permute-start | bytes 589832 | tf_op jit(solution)/shard_map/ppermute | solution.py:18
  20.1 47.6 %collective-permute-start = (f32[6,16,4,128]{3,1,2,0:T(8,128)}, f32[6,16,4,128]{3,1,2,0:T(8,128)}, u32[]{:S(2)}, u32[]{:S(2)}) collective-permute-start(f32[6,16,4,128]{3,1,2,0:T(8,128)} %copy.199), channel_id=1, source_target_pairs={{0,16},{16,32},{32,48},{48,64},{64,80},{80,96},{96,112},{1,17},{17... | collective-permute-start | bytes 589832 | tf_op jit(solution)/shard_map/ppermute | solution.py:17
  28.2 12.8 %all-to-all-start = ((f32[8,1,4608]{2,1,0:T(1,128)}), f32[8,1,4608]{2,1,0:T(1,128)S(1)}, u32[]{:S(2)}, u32[]{:S(2)}) async-start(f32[8,1,4608]{2,1,0:T(1,128)} %reshape.99), calls=%async_computation | async-start | bytes 294912 | tf_op jit(solution)/shard_map/all_to_all | solution.py:125
  41.0 39.4 %all-to-all-start.4 = ((f32[16,1,2304]{2,1,0:T(1,128)}), f32[16,1,2304]{2,1,0:T(1,128)S(1)}, u32[]{:S(2)}, u32[]{:S(2)}) async-start(f32[16,1,2304]{2,1,0:T(1,128)} %reshape.95), calls=%async_computation.4 | async-start | bytes 294912 | tf_op jit(solution)/shard_map/all_to_all | solution.py:124
  75.0 52.4 %collective-permute-start.3 = (f32[6,16,72,4]{2,1,3,0:T(8,128)}, f32[6,16,72,4]{2,1,3,0:T(8,128)S(1)}, u32[]{:S(2)}, u32[]{:S(2)}) collective-permute-start(f32[6,16,72,4]{2,1,3,0:T(8,128)} %get-tuple-element.37), channel_id=1, source_target_pairs={{1,0},{2,1},{3,2},{4,3},{5,4},{6,5},{7,6},{8,7},{9,8},{10,9},{11,1... | collective-permute-start | bytes 331784 | tf_op jit(solution)/shard_map/ppermute | solution.py:18
  78.4 49.0 %collective-permute-start.2 = (f32[6,16,72,4]{2,1,3,0:T(8,128)S(1)}, f32[6,16,72,4]{2,1,3,0:T(8,128)}, u32[]{:S(2)}, u32[]{:S(2)}) collective-permute-start(f32[6,16,72,4]{2,1,3,0:T(8,128)S(1)} %get-tuple-element.36), channel_id=1, source_target_pairs={{0,1},{1,2},{2,3},{3,4},{4,5},{5,6},{6,7},{7,8},{8,9},{9,10},{10,1... | collective-permute-start | bytes 331784 | tf_op jit(solution)/shard_map/ppermute | solution.py:17
  91.5 11.6 %all-to-all-start.5 = ((f32[8,1,4608]{2,1,0:T(1,128)}), f32[8,1,4608]{2,1,0:T(1,128)S(1)}, u32[]{:S(2)}, u32[]{:S(2)}) async-start(f32[8,1,4608]{2,1,0:T(1,128)} %reshape.97), calls=%async_computation.5 | async-start | bytes 294912 | tf_op jit(solution)/shard_map/all_to_all | solution.py:131
  103.1 12.0 %all-to-all-start.2 = ((f32[8,1,4608]{2,1,0:T(1,128)}), f32[8,1,4608]{2,1,0:T(1,128)S(1)}, u32[]{:S(2)}, u32[]{:S(2)}) async-start(f32[8,1,4608]{2,1,0:T(1,128)} %reshape.103), calls=%async_computation.2 | async-start | bytes 294912 | tf_op jit(solution)/shard_map/all_to_all | solution.py:131
  120.2 13.7 %collective-permute-start.5 = (f32[36,1,64]{2,1,0:T(1,128)S(1)}, f32[36,1,64]{2,1,0:T(1,128)S(1)}, u32[]{:S(2)}, u32[]{:S(2)}) collective-permute-start(f32[36,1,64]{2,1,0:T(1,128)S(1)} %get-tuple-element.98), channel_id=1, source_target_pairs={{16,0},{32,16},{48,32},{64,48},{80,64},{96,80},{112,96},{17,1},{33... | collective-permute-start | bytes 27656 | tf_op jit(solution)/shard_map/ppermute | solution.py:18
  138.2 11.3 %collective-permute-start.7 = (f32[36,34,1]{0,2,1:T(1,128)}, f32[36,34,1]{0,2,1:T(1,128)}, u32[]{:S(2)}, u32[]{:S(2)}) collective-permute-start(f32[36,34,1]{0,2,1:T(1,128)} %copy.164), channel_id=1, source_target_pairs={{1,0},{2,1},{3,2},{4,3},{5,4},{6,5},{7,6},{8,7},{9,8},{10,9},{11,1... | collective-permute-start | bytes 14696 | tf_op jit(solution)/shard_map/ppermute | solution.py:18
  215.9 13.4 %collective-permute-start.9 = (f32[3,16,4,128]{3,1,2,0:T(8,128)S(1)}, f32[3,16,4,128]{3,1,2,0:T(8,128)S(1)}, u32[]{:S(2)}, u32[]{:S(2)}) collective-permute-start(f32[3,16,4,128]{3,1,2,0:T(8,128)S(1)} %copy.173), channel_id=1, source_target_pairs={{16,0},{32,16},{48,32},{64,48},{80,64},{96,80},{112,96},{17,1},{33... | collective-permute-start | bytes 294920 | tf_op jit(solution)/shard_map/ppermute | solution.py:18
  303.0 11.9 %collective-permute-start.13 = (f32[6,16,4,128]{3,1,2,0:T(8,128)S(1)}, f32[6,16,4,128]{3,1,2,0:T(8,128)S(1)}, u32[]{:S(2)}, u32[]{:S(2)}) collective-permute-start(f32[6,16,4,128]{3,1,2,0:T(8,128)S(1)} %copy.179), channel_id=1, source_target_pairs={{16,0},{32,16},{48,32},{64,48},{80,64},{96,80},{112,96},{17,1},{33... | collective-permute-start | bytes 589832 | tf_op jit(solution)/shard_map/ppermute | solution.py:18
  417.2 14.0 %collective-permute-start.19 = (f32[3,16,72,4]{2,1,3,0:T(8,128)}, f32[3,16,72,4]{2,1,3,0:T(8,128)}, u32[]{:S(2)}, u32[]{:S(2)}) collective-permute-start(f32[3,16,72,4]{2,1,3,0:T(8,128)} %get-tuple-element.45), channel_id=1, source_target_pairs={{1,0},{2,1},{3,2},{4,3},{5,4},{6,5},{7,6},{8,7},{9,8},{10,9},{11,1... | collective-permute-start | bytes 165896 | tf_op jit(solution)/shard_map/ppermute | solution.py:18
  419.1 12.1 %collective-permute-start.18 = (f32[3,16,72,4]{2,1,3,0:T(8,128)}, f32[3,16,72,4]{2,1,3,0:T(8,128)}, u32[]{:S(2)}, u32[]{:S(2)}) collective-permute-start(f32[3,16,72,4]{2,1,3,0:T(8,128)} %get-tuple-element.44), channel_id=1, source_target_pairs={{0,1},{1,2},{2,3},{3,4},{4,5},{5,6},{6,7},{7,8},{8,9},{9,10},{10,1... | collective-permute-start | bytes 165896 | tf_op jit(solution)/shard_map/ppermute | solution.py:17
  559.5 33.6 %all-to-all-start.7 = ((f32[16,1,4608]{2,1,0:T(1,128)}), f32[16,1,4608]{2,1,0:T(1,128)}, u32[]{:S(2)}, u32[]{:S(2)}) async-start(f32[16,1,4608]{2,1,0:T(1,128)} %reshape.107), calls=%async_computation.7 | async-start | bytes 589824 | tf_op jit(solution)/shard_map/all_to_all | solution.py:124
  565.7 13.8 %collective-permute-start.21 = (f32[6,8,16,4]{3,2,1,0:T(8,128)S(1)}, f32[6,8,16,4]{3,2,1,0:T(8,128)S(1)}, u32[]{:S(2)}, u32[]{:S(2)}) collective-permute-start(f32[6,8,16,4]{3,2,1,0:T(8,128)S(1)} %get-tuple-element.96), channel_id=1, source_target_pairs={{16,0},{32,16},{48,32},{64,48},{80,64},{96,80},{112,96},{17,1},{33... | collective-permute-start | bytes 36872 | tf_op jit(solution)/shard_map/ppermute | solution.py:18
  570.8 16.4 %collective-permute-start.20 = (f32[6,8,16,4]{3,2,1,0:T(8,128)S(1)}, f32[6,8,16,4]{3,2,1,0:T(8,128)S(1)}, u32[]{:S(2)}, u32[]{:S(2)}) collective-permute-start(f32[6,8,16,4]{3,2,1,0:T(8,128)S(1)} %get-tuple-element.95), channel_id=1, source_target_pairs={{0,16},{16,32},{32,48},{48,64},{64,80},{80,96},{96,112},{1,17},{17... | collective-permute-start | bytes 36872 | tf_op jit(solution)/shard_map/ppermute | solution.py:17
  588.4 20.7 %collective-permute-start.23 = (f32[6,8,4,136]{3,2,1,0:T(4,128)}, f32[6,8,4,136]{3,2,1,0:T(4,128)}, u32[]{:S(2)}, u32[]{:S(2)}) collective-permute-start(f32[6,8,4,136]{3,2,1,0:T(4,128)} %get-tuple-element.83), channel_id=1, source_target_pairs={{1,0},{2,1},{3,2},{4,3},{5,4},{6,5},{7,6},{8,7},{9,8},{10,9},{11,1... | collective-permute-start | bytes 313352 | tf_op jit(solution)/shard_map/ppermute | solution.py:18
  591.2 17.8 %collective-permute-start.22 = (f32[6,8,4,136]{3,2,1,0:T(4,128)}, f32[6,8,4,136]{3,2,1,0:T(4,128)}, u32[]{:S(2)}, u32[]{:S(2)}) collective-permute-start(f32[6,8,4,136]{3,2,1,0:T(4,128)} %get-tuple-element.82), channel_id=1, source_target_pairs={{0,1},{1,2},{2,3},{3,4},{4,5},{5,6},{6,7},{7,8},{8,9},{9,10},{10,1... | collective-permute-start | bytes 313352 | tf_op jit(solution)/shard_map/ppermute | solution.py:17
  602.7 12.5 %all-to-all-start.8 = ((f32[8,1,9216]{2,1,0:T(1,128)}), f32[8,1,9216]{2,1,0:T(1,128)}, u32[]{:S(2)}, u32[]{:S(2)}) async-start(f32[8,1,9216]{2,1,0:T(1,128)} %reshape.109), calls=%async_computation.8 | async-start | bytes 589824 | tf_op jit(solution)/shard_map/all_to_all | solution.py:131
  634.4 12.1 %collective-permute-start.24 = (f32[3,8,16,4]{3,2,1,0:T(8,128)S(1)}, f32[3,8,16,4]{3,2,1,0:T(8,128)S(1)}, u32[]{:S(2)}, u32[]{:S(2)}) collective-permute-start(f32[3,8,16,4]{3,2,1,0:T(8,128)S(1)} %get-tuple-element.99), channel_id=1, source_target_pairs={{0,16},{16,32},{32,48},{48,64},{64,80},{80,96},{96,112},{1,17},{17... | collective-permute-start | bytes 18440 | tf_op jit(solution)/shard_map/ppermute | solution.py:17
  648.1 21.4 %collective-permute-start.27 = (f32[3,8,4,136]{3,2,1,0:T(4,128)}, f32[3,8,4,136]{3,2,1,0:T(4,128)}, u32[]{:S(2)}, u32[]{:S(2)}) collective-permute-start(f32[3,8,4,136]{3,2,1,0:T(4,128)} %get-tuple-element.94), channel_id=1, source_target_pairs={{1,0},{2,1},{3,2},{4,3},{5,4},{6,5},{7,6},{8,7},{9,8},{10,9},{11,1... | collective-permute-start | bytes 156680 | tf_op jit(solution)/shard_map/ppermute | solution.py:18
  650.2 19.3 %collective-permute-start.26 = (f32[3,8,4,136]{3,2,1,0:T(4,128)}, f32[3,8,4,136]{3,2,1,0:T(4,128)}, u32[]{:S(2)}, u32[]{:S(2)}) collective-permute-start(f32[3,8,4,136]{3,2,1,0:T(4,128)} %get-tuple-element.93), channel_id=1, source_target_pairs={{0,1},{1,2},{2,3},{3,4},{4,5},{5,6},{6,7},{7,8},{8,9},{9,10},{10,1... | collective-permute-start | bytes 156680 | tf_op jit(solution)/shard_map/ppermute | solution.py:17
  (76 other events, 677.1 us)
where the time goes:
time: 687 us; the launch traced here: 675 us
  other arithmetic  256 us (37%)
  local copies, waits for them, and re-layouts  222 us (32%)
  starting transfers between devices  134 us (20%)
  waiting for transfers between devices  49.3 us (7%)
  blocking collectives  11.7 us (2%)
    unnamed x154, local copies, waits for them, and re-layouts  69.5 us
    ppermute x14, starting transfers between devices, extended(): after = lax.ppermute(leading, axis, down)  52.4 us
    another operation x9, other arithmetic, velocity_step(): jnp.stack([first_rate, second_rate, third_rate])  46.2 us
    unnamed x20, other arithmetic  42.1 us
    concatenate x4, other arithmetic, below_pad(): jnp.concatenate([zero_layers(widened, 4), widened, widen_ghost(widened, g...  35.9 us
    ppermute x14, waiting for transfers between devices, extended(): before = lax.ppermute(last, axis, up)  33.7 us
    ppermute x14, starting transfers between devices, extended(): before = lax.ppermute(last, axis, up)  30.3 us
    slice x11, local copies, waits for them, and re-layouts, extended(): last = lax.slice_in_dim(x, length - width, length, axis=dim)  27.7 us
  transfers between devices with their start and end apart: 36, of which 16 were waited for; matrix products, arithmetic and copies ran while one was open for 21% of the time, Pallas kernels for 0%

commit v1 on v0

v1 whole, which is shorter than its diff:
```python
import jax
import jax.numpy as jnp
from jax import lax
from jax.experimental import pallas as pl
from jax.experimental.pallas import tpu as pltpu
from jax.sharding import PartitionSpec as P

C = (1225.0 / 1024.0, -245.0 / 3072.0, 49.0 / 5120.0, -5.0 / 7168.0)
SCALE = 0.1
MESH = pl.DeviceIdType.MESH
HI = lax.Precision.HIGHEST
F32 = jnp.float32

SX, SY, SYSIGN = (0, 3, 4), (3, 1, 5), (False, True, False)
VX, VY, VYSIGN = (0, 1, 2), (0, 1, 2), (True, False, True)


def lanes(shape):
    return lax.broadcasted_iota(jnp.int32, shape, len(shape) - 1)


def shifted(f, s):
    return f if s == 0 else pltpu.roll(f, (-s) % 128, f.ndim - 1)


def taps(get, fwd):
    out = None
    for k in range(1, 5):
        hi, lo = (k, 1 - k) if fwd else (k - 1, -k)
        term = C[k - 1] * (get(hi) - get(lo))
        out = term if out is None else out + term
    return out


def d_rows(buf, f, zz, r0, nr, fwd):
    return taps(lambda s: buf[f, zz, 8 + r0 + s : 8 + r0 + s + nr, :], fwd)


def d_layers(buf, f, zz, r0, nr, fwd):
    return taps(lambda s: buf[f, zz + s, 8 + r0 : 8 + r0 + nr, :], fwd)


def d_cols(buf, f, slot, corr, zz, zl, r0, nr, fwd):
    here = buf[f, zz, 8 + r0 : 8 + r0 + nr, :]
    inner = taps(lambda s: shifted(here, s), fwd)
    at = slot * 32 + zl * 4
    right = pltpu.roll(corr[0, r0 : r0 + nr, :], lax.rem(252 - at, 128), 1)
    left = pltpu.roll(corr[1, r0 : r0 + nr, :], lax.rem(256 - at, 128), 1)
    lane = lanes((nr, 128))
    edge = jnp.where(lane >= 124, right, jnp.where(lane < 4, left, 0.0))
    return inner + edge


def edge_weight(s, side, signs):
    lane = lanes((8, 128))
    j, field = lane & 3, lane >> 5
    inside = (j + s >= 0) & (j + s <= 3)

    def weight(fwd):
        if side == 0:
            k = (4 if fwd else 5) + s
            return C[k - 1] if 1 <= k <= 4 else 0.0
        k = (5 if fwd else 4) - s
        return -C[k - 1] if 1 <= k <= 4 else 0.0

    w = jnp.where(field == 0, weight(signs[0]), jnp.where(field == 1, weight(signs[1]), weight(signs[2])))
    return jnp.where(inside & (field < 3), w, 0.0)


def make_corr(corr, own, got, signs, nrow):
    for side in range(2):
        shifts = (0, -1, -2, -3) if side == 0 else (0, 1, 2, 3)
        weights = [edge_weight(s, side, signs) for s in shifts]

        def body(r, carry, side=side, shifts=shifts, weights=weights):
            rows = pl.ds(pl.multiple_of(r * 8, 8), 8)
            miss = got[1 - side, rows, :] - own[side, rows, :]
            total = None
            for s, w in zip(shifts, weights):
                term = w * shifted(miss, s)
                total = term if total is None else total + term
            corr[side, rows, :] = total
            return carry

        lax.fori_loop(0, nrow // 8, body, 0)


def pack_rows(buf, out, fields, z0, nrow):
    for i, f in enumerate(fields):
        for zl in range(8):
            half = 4 * (zl % 2)
            out[0, i, zl // 2, half : half + 4, :] = buf[f, 4 + z0 + zl, 8:12, :]
            out[1, i, zl // 2, half : half + 4, :] = buf[f, 4 + z0 + zl, 4 + nrow : 8 + nrow, :]


def unpack_rows(buf, got, fields, z0, nrow):
    for i, f in enumerate(fields):
        for zl in range(8):
            half = 4 * (zl % 2)
            buf[f, 4 + z0 + zl, 4:8, :] = got[0, i, zl // 2, half : half + 4, :]
            buf[f, 4 + z0 + zl, 8 + nrow : 12 + nrow, :] = got[1, i, zl // 2, half : half + 4, :]


def pack_cols(buf, out, fields, z0, nrow):
    lane = lanes((8, 128))

    def body(r, carry):
        src = pl.ds(pl.multiple_of(r * 8 + 8, 8), 8)
        first = jnp.zeros((8, 128), F32)
        last = jnp.zeros((8, 128), F32)
        for i, f in enumerate(fields):
            for zl in range(8):
                at = i * 32 + zl * 4
                here = buf[f, 4 + z0 + zl, src, :]
                mine = (lane >> 2) == (at >> 2)
                first = jnp.where(mine, shifted(here, -at), first)
                last = jnp.where(mine, shifted(here, 124 - at), last)
        dst = pl.ds(pl.multiple_of(r * 8, 8), 8)
        out[0, dst, :] = first
        out[1, dst, :] = last
        return carry

    lax.fori_loop(0, nrow // 8, body, 0)


def velocity_update(vb, sb, mb, corr, z0, n, nrow, zl0=0):
    nr = min(nrow, 16)

    def body(i, carry):
        zl = i + zl0
        z = z0 + zl
        zz = z + 4
        for r0 in range(0, nrow, nr):
            rows = slice(8 + r0, 8 + r0 + nr)
            b = mb[0, z, r0 : r0 + nr, :] * SCALE
            cols = lambda f, slot, fwd: d_cols(sb, f, slot, corr, zz, zl, r0, nr, fwd)
            row = lambda f, fwd: d_rows(sb, f, zz, r0, nr, fwd)
            lay = lambda f, fwd: d_layers(sb, f, zz, r0, nr, fwd)
            vb[0, zz, rows, :] = vb[0, zz, rows, :] + b * (row(0, True) + cols(3, 0, False) + lay(4, False))
            vb[1, zz, rows, :] = vb[1, zz, rows, :] + b * (row(3, False) + cols(1, 1, True) + lay(5, False))
            vb[2, zz, rows, :] = vb[2, zz, rows, :] + b * (row(4, False) + cols(5, 2, False) + lay(2, True))
        return carry

    lax.fori_loop(0, n, body, 0)


def stress_update(vb, sb, mb, corr, z0, n, nrow, zl0=0):
    nr = min(nrow, 16)

    def body(i, carry):
        zl = i + zl0
        z = z0 + zl
        zz = z + 4
        for r0 in range(0, nrow, nr):
            rows = slice(8 + r0, 8 + r0 + nr)
            lam = mb[1, z, r0 : r0 + nr, :] * SCALE
            mu = mb[2, z, r0 : r0 + nr, :] * SCALE
            cols = lambda f, fwd: d_cols(vb, f, f, corr, zz, zl, r0, nr, fwd)
            row = lambda f, fwd: d_rows(vb, f, zz, r0, nr, fwd)
            lay = lambda f, fwd: d_layers(vb, f, zz, r0, nr, fwd)
            exx, eyy, ezz = row(0, False), cols(1, False), lay(2, False)
            dil = lam * (exx + eyy + ezz)
            two = mu + mu
            sb[0, zz, rows, :] = sb[0, zz, rows, :] + (dil + two * exx)
            sb[1, zz, rows, :] = sb[1, zz, rows, :] + (dil + two * eyy)
            sb[2, zz, rows, :] = sb[2, zz, rows, :] + (dil + two * ezz)
            sb[3, zz, rows, :] = sb[3, zz, rows, :] + mu * (cols(0, True) + row(1, True))
            sb[4, zz, rows, :] = sb[4, zz, rows, :] + mu * (lay(0, True) + row(2, True))
            sb[5, zz, rows, :] = sb[5, zz, rows, :] + mu * (lay(1, True) + cols(2, True))
        return carry

    lax.fori_loop(0, n, body, 0)


N_MSG = 64
ID_FINE, ID_CS, ID_CV, ID_MAIN, ID_FAR, ID_ROW, ID_KNOT, ID_LIFT = 0, 32, 36, 40, 42, 44, 46, 48


def kernel(
    nx, ny, fs, fm, cs, cm, cp, prow, pcol, fout, cout,
    vb, sb, mb, old, xs, xr, ys, yr, corr,
    cvb, csb, cmb, cpb, cxs, cxr, cys, cyr, ccorr,
    send_main, send_far, send_row, send_knot, got_main, got_far, got_row, got_knot,
    stack, wide, planes, half, pairs, send_lift, got_lift,
    send_sem, recv_sem, load_sem, out_sem,
):
    gx = lax.axis_index("gx")
    gy = lax.axis_index("gy")
    up, down = gx > 0, gx < nx - 1
    left, right = gy > 0, gy < ny - 1
    oc, par = gy // 2, lax.rem(gy, 2)
    even = par == 0
    far_c = jnp.where(even, oc - 1, oc + 1)
    has_far = jnp.logical_and(far_c >= 0, far_c <= nx - 1)
    slot_out = 1 - par
    row_t = oc + 2 * par - 1
    has_row_t = jnp.logical_and(row_t >= 0, row_t <= nx - 1)

    def is_me(t):
        return jnp.logical_and(t[0] == gx, t[1] == gy)

    true = gx >= 0
    sent = []

    def send(src, dst, sid, rid, target, cond, maybe_self=False):
        remote = jnp.logical_and(cond, jnp.logical_not(is_me(target))) if maybe_self else cond

        def copy():
            return pltpu.make_async_remote_copy(
                src_ref=src, dst_ref=dst, send_sem=send_sem.at[sid], recv_sem=recv_sem.at[rid],
                device_id=target, device_id_type=MESH,
            )

        @pl.when(remote)
        def _():
            copy().start()

        if maybe_self:

            @pl.when(jnp.logical_and(cond, is_me(target)))
            def _():
                pltpu.make_async_copy(src, dst, recv_sem.at[rid]).start()

        sent.append((remote, copy))

    def receive(dst, rid, cond=None):
        def wait():
            pltpu.make_async_copy(dst, dst, recv_sem.at[rid]).wait()

        if cond is None:
            wait()
        else:
            pl.when(cond)(wait)

    loads = [
        pltpu.make_async_copy(cs.at[0:3], cvb.at[:, 4:12, 8:24, :], load_sem.at[0]),
        pltpu.make_async_copy(cs.at[3:9], csb.at[:, 4:12, 8:24, :], load_sem.at[1]),
        pltpu.make_async_copy(cp, cpb, load_sem.at[2]),
        pltpu.make_async_copy(fs.at[3:9], sb.at[:, 4:20, 8:72, :], load_sem.at[3]),
        pltpu.make_async_copy(fs.at[0:3], vb.at[:, 4:20, 8:72, :], load_sem.at[4]),
        pltpu.make_async_copy(fm, mb, load_sem.at[5]),
        pltpu.make_async_copy(fs.at[0:3, 8:16], old.at[0:3], load_sem.at[6]),
        pltpu.make_async_copy(fs.at[5, 8:16], old.at[3], load_sem.at[7]),
        pltpu.make_async_copy(fs.at[7:9, 8:16], old.at[4:6], load_sem.at[8]),
        pltpu.make_async_copy(cm, cmb, load_sem.at[9]),
    ]
    for load in loads:
        load.start()

    barrier = pltpu.get_barrier_semaphore()

    def greet(target, cond, maybe_self=False):
        if maybe_self:
            cond = jnp.logical_and(cond, jnp.logical_not(is_me(target)))

        @pl.when(cond)
        def _():
            pl.semaphore_signal(barrier, inc=1, device_id=target, device_id_type=MESH)

    def count(target, cond, maybe_self=False):
        if maybe_self:
            cond = jnp.logical_and(cond, jnp.logical_not(is_me(target)))
        return jnp.where(cond, 1, 0)

    near = [((gx - 1, gy), up), ((gx + 1, gy), down), ((gx, gy - 1), left), ((gx, gy + 1), right)]
    owners = [(oc, 2 * gx), (oc, 2 * gx + 1)]
    for target, cond in near:
        greet(target, cond)
    for target in owners:
        greet(target, true, True)
        greet((far_c, target[1]), has_far)
    top_ok, bot_ok = up, down
    greet((oc, 2 * gx - 1), top_ok)
    greet((oc, 2 * gx + 2), bot_ok)
    greet((far_c, 2 * gx - 1), jnp.logical_and(top_ok, has_far), True)
    greet((far_c, 2 * gx + 2), jnp.logical_and(bot_ok, has_far), True)

    a = oc
    main_t = owners
    far_t = [((a, 2 * gx - 1), gx > 0), ((a, 2 * gx + 2), gx < nx - 1)]
    row_ts = [((row_t, 2 * gx), has_row_t), ((row_t, 2 * gx + 1), has_row_t)]
    knot_t = [
        ((row_t, 2 * gx - 1), jnp.logical_and(has_row_t, gx > 0)),
        ((row_t, 2 * gx + 2), jnp.logical_and(has_row_t, gx < nx - 1)),
    ]
    expected = jnp.int32(0)
    for target, cond in near:
        expected = expected + count(target, cond)
    for target in owners:
        expected = expected + count(target, true, True)
    for target, cond in far_t:
        expected = expected + count(target, cond)
    for target, cond in row_ts:
        expected = expected + count(target, cond)
    for target, cond in knot_t:
        expected = expected + count(target, cond, True)

    def clear(ref):
        ref[...] = jnp.zeros(ref.shape, F32)

    for cond, row_slot in ((up, 0), (down, 1)):

        @pl.when(jnp.logical_not(cond))
        def _(row_slot=row_slot):
            for e in range(8):
                clear(xr.at[e, row_slot])
            for e in range(2):
                clear(cyr.at[e, row_slot])

    for cond, col_slot in ((left, 0), (right, 1)):

        @pl.when(jnp.logical_not(cond))
        def _(col_slot=col_slot):
            for e in range(8):
                clear(yr.at[e, col_slot])
            for e in range(2):
                clear(cxr.at[e, col_slot])

    for f in range(3):
        vb[f, 0:4, 8:72, :] = jnp.zeros((4, 64, 128), F32)
        cvb[f, 12:16, 8:24, :] = jnp.zeros((4, 16, 128), F32)
    for f in (2, 4, 5):
        sb[f, 0:4, 8:72, :] = jnp.zeros((4, 64, 128), F32)
        csb[f, 12:16, 8:24, :] = jnp.zeros((4, 16, 128), F32)

    @pl.when(jnp.logical_not(has_far))
    def _():
        clear(got_far)

    for slot, cond in ((0, up), (1, down)):

        @pl.when(jnp.logical_not(jnp.logical_and(cond, has_far)))
        def _(slot=slot):
            clear(got_knot.at[slot])

    loads[0].wait()
    loads[1].wait()
    loads[2].wait()
    lane16 = lanes((16, 128))
    low = lane16 < 64
    tile_near = [jnp.zeros((16, 128), F32), jnp.zeros((16, 128), F32)]
    tile_far = [jnp.zeros((16, 128), F32), jnp.zeros((16, 128), F32)]
    for s in range(2):
        for f6 in range(6):
            p = s * 6 + f6
            buf, f, fp = (cvb, f6, f6) if f6 < 3 else (csb, (2, 4, 5)[f6 - 3], (5, 7, 8)[f6 - 3])
            layer = []
            for m in range(2):
                plane = buf[f, 4 + m, 8:24, :]
                if s == 1:
                    plane = 1.5 * plane - 0.5 * cpb[fp, m, :, :]
                layer.append(plane)
                q = 2 * p + m
                here = lane16 == q
                tile_near[0] = jnp.where(here, shifted(plane, 64 - q), tile_near[0])
                tile_near[1] = jnp.where(here, shifted(plane, 63 - q), tile_near[1])
                tile_far[0] = jnp.where(here, shifted(plane, -q), tile_far[0])
                tile_far[1] = jnp.where(here, shifted(plane, 127 - q), tile_far[1])
            send_main[0, p, :, :] = jnp.where(low, layer[0], shifted(layer[1], 64))
            send_main[1, p, :, :] = jnp.where(low, shifted(layer[0], 64), layer[1])
    for side in range(2):
        send_main[side, 12, :, :] = tile_near[side]
        send_far[side, :, :] = tile_far[side]

    for dd, row in ((0, 0), (1, 15)):

        @pl.when(par == dd)
        def _(row=row):
            for side in range(2):
                for p in range(13):
                    send_row[side, p : p + 1, :] = send_main[side, p, row : row + 1, :]
                send_knot[side, 0:1, :] = send_far[side, row : row + 1, :]

    pl.semaphore_wait(barrier, expected)

    for side in range(2):
        send(send_main.at[side], got_main.at[par], ID_MAIN + side, ID_MAIN + par, main_t[side], true, True)
        send(send_far.at[side], got_far.at[par], ID_FAR + side, ID_FAR + par, *far_t[side])
        send(send_row.at[side], got_row.at[slot_out], ID_ROW + side, ID_ROW + slot_out, *row_ts[side])
        send(send_knot.at[side], got_knot.at[slot_out], ID_KNOT + side, ID_KNOT + slot_out, *knot_t[side], True)

    def fine_send(e, ch, buf, xf, yf):
        m = 2 * e + ch
        pack_rows(buf, xs.at[m], xf, 8 * ch, 64)
        pack_cols(buf, ys.at[m], yf, 8 * ch, 64)
        i = ID_FINE + 4 * m
        send(xs.at[m, 0], xr.at[m, 1], i, i + 1, *near[0])
        send(xs.at[m, 1], xr.at[m, 0], i + 1, i, *near[1])
        send(ys.at[m, 0], yr.at[m, 1], i + 2, i + 3, *near[2])
        send(ys.at[m, 1], yr.at[m, 0], i + 3, i + 2, *near[3])

    def fine_receive(e, ch, buf, xf, signs):
        m = 2 * e + ch
        i = ID_FINE + 4 * m
        receive(xr.at[m, 0], i, up)
        receive(xr.at[m, 1], i + 1, down)
        unpack_rows(buf, xr.at[m], xf, 8 * ch, 64)
        receive(yr.at[m, 0], i + 2, left)
        receive(yr.at[m, 1], i + 3, right)
        make_corr(corr, ys.at[m], yr.at[m], signs, 64)

    def coarse_send(e, buf, xf, yf):
        pack_rows(buf, cxs.at[e], xf, 0, 16)
        pack_cols(buf, cys.at[e], yf, 0, 16)
        i = ID_CS + 4 * e
        send(cxs.at[e, 0], cxr.at[e, 1], i, i + 1, *near[2])
        send(cxs.at[e, 1], cxr.at[e, 0], i + 1, i, *near[3])
        send(cys.at[e, 0], cyr.at[e, 1], i + 2, i + 3, *near[0])
        send(cys.at[e, 1], cyr.at[e, 0], i + 3, i + 2, *near[1])

    def coarse_receive(e, buf, xf, signs):
        i = ID_CS + 4 * e
        receive(cxr.at[e, 0], i, left)
        receive(cxr.at[e, 1], i + 1, right)
        unpack_rows(buf, cxr.at[e], xf, 0, 16)
        receive(cyr.at[e, 0], i + 2, up)
        receive(cyr.at[e, 1], i + 3, down)
        make_corr(ccorr, cys.at[e], cyr.at[e], signs, 16)

    loads[3].wait()
    fine_send(0, 0, sb, SX, SY)
    fine_send(0, 1, sb, SX, SY)
    coarse_send(0, csb, SX, SY)
    loads[4].wait()
    loads[5].wait()

    fine_receive(0, 0, sb, SX, SYSIGN)
    velocity_update(vb, sb, mb, corr, 0, 8, 64)
    fine_send(1, 0, vb, VX, VY)

    receive(got_main.at[0], ID_MAIN)
    receive(got_main.at[1], ID_MAIN + 1)
    receive(got_far.at[0], ID_FAR, has_far)
    receive(got_far.at[1], ID_FAR + 1, has_far)
    receive(got_row.at[0], ID_ROW, top_ok)
    receive(got_row.at[1], ID_ROW + 1, bot_ok)
    receive(got_knot.at[0], ID_KNOT, jnp.logical_and(top_ok, has_far))
    receive(got_knot.at[1], ID_KNOT + 1, jnp.logical_and(bot_ok, has_far))
    for h in range(2):
        for p in range(13):
            stack[p, 1 + 16 * h : 17 + 16 * h, :] = got_main[h, p, :, :]
        stack[13, 1 + 16 * h : 17 + 16 * h, :] = got_far[h, :, :]

    for h, row, src_row, ok in ((0, 0, 0, top_ok), (1, 33, 15, bot_ok)):

        @pl.when(ok)
        def _(h=h, row=row):
            for p in range(13):
                stack[p, row : row + 1, :] = got_row[h, p : p + 1, :]
            stack[13, row : row + 1, :] = got_knot[h, 0:1, :]

        @pl.when(jnp.logical_not(ok))
        def _(h=h, row=row, src_row=src_row):
            for p in range(13):
                stack[p, row : row + 1, :] = got_main[h, p, src_row : src_row + 1, :]
            stack[13, row : row + 1, :] = got_far[h, src_row : src_row + 1, :]

    row16 = lax.broadcasted_iota(jnp.int32, (16, 128), 0)
    flips = jnp.zeros((16, 128), jnp.int32)
    for k in range(16):
        flips = jnp.where(row16 == k, prow[4 * k + 1] - gx * 32 - 2 * k, flips)
    flipped = flips == 1
    for p in range(14):
        wide[p, pl.ds(0, 16, stride=4), :] = stack[p, pl.ds(0, 16, stride=2), :]
        wide[p, pl.ds(1, 16, stride=4), :] = jnp.where(
            flipped, stack[p, pl.ds(2, 16, stride=2), :], stack[p, pl.ds(1, 16, stride=2), :]
        )
        wide[p, pl.ds(2, 16, stride=4), :] = stack[p, pl.ds(2, 16, stride=2), :]
        wide[p, pl.ds(3, 16, stride=4), :] = stack[p, pl.ds(3, 16, stride=2), :]

    col = jnp.clip(pcol[...].reshape(1, 128) - gy * 64, 0, 63)
    src_lane = lax.broadcasted_iota(jnp.int32, (128, 128), 0)
    pick0 = jnp.where(src_lane == col, 1.0, 0.0).astype(F32)
    pick1 = jnp.where(src_lane == col + 64, 1.0, 0.0).astype(F32)
    pick = jnp.concatenate([pick0, pick1], axis=1)
    lane64 = lanes((64, 128))
    at_first = jnp.logical_and(lane64 == 0, left)
    at_last = jnp.logical_and(lane64 == 127, right)

    first_ring = jnp.where(even, wide[13, :, :], wide[12, :, :])
    last_ring = jnp.where(even, wide[12, :, :], wide[13, :, :])
    half[0, :, :] = first_ring
    half[1, :, :] = last_ring

    def expand(p, carry):
        both = jnp.dot(wide[p, :, :], pick, precision=HI, preferred_element_type=F32)
        for m in range(2):
            plane = both[:, 128 * m : 128 * m + 128]
            q = 2 * p + m
            one = pltpu.roll(half[0, :, :], lax.rem(128 - q, 128), 1)
            two = pltpu.roll(half[1, :, :], 127 - q, 1)
            planes[q, :, :] = jnp.where(at_first, one, jnp.where(at_last, two, plane))
        return carry

    lax.fori_loop(0, 12, expand, 0)

    def place(s):
        for f6 in range(6):
            buf, f = (vb, f6) if f6 < 3 else (sb, (2, 4, 5)[f6 - 3])
            for g in range(4):
                buf[f, 20 + g, 8:72, :] = planes[2 * (s * 6 + f6) + g // 2, :, :]

    place(0)

    fine_receive(0, 1, sb, SX, SYSIGN)
    velocity_update(vb, sb, mb, corr, 8, 8, 64)
    fine_send(1, 1, vb, VX, VY)
    coarse_receive(0, csb, SX, SYSIGN)

    fine_receive(1, 0, vb, VX, VYSIGN)
    stress_update(vb, sb, mb, corr, 0, 8, 64)
    fine_send(2, 0, sb, SX, SY)
    fine_receive(1, 1, vb, VX, VYSIGN)
    stress_update(vb, sb, mb, corr, 8, 8, 64)
    fine_send(2, 1, sb, SX, SY)
    place(1)

    outs = []

    def emit(src, dst):
        copy = pltpu.make_async_copy(src, dst, out_sem.at[len(outs)])
        copy.start()
        outs.append(copy)

    fine_receive(2, 0, sb, SX, SYSIGN)
    velocity_update(vb, sb, mb, corr, 0, 8, 64)
    fine_send(3, 0, vb, VX, VY)
    fine_receive(2, 1, sb, SX, SYSIGN)
    velocity_update(vb, sb, mb, corr, 8, 8, 64)
    fine_send(3, 1, vb, VX, VY)
    emit(vb.at[:, 4:20, 8:72, :], fout.at[0:3])

    tgt_lane = lanes((128, 128))
    even_pick = jnp.where(tgt_lane == src_lane // 2, 0.0625, 0.0).astype(F32)
    odd_pick = jnp.where(tgt_lane == 64 + src_lane // 2, 0.0625, 0.0).astype(F32)

    def lift(kind, buf, fields):
        for i, f in enumerate(fields):
            for m in range(4):
                half[0, :, :] = (
                    old[3 * kind + i, 2 * m, :, :] + old[3 * kind + i, 2 * m + 1, :, :]
                    + buf[f, 12 + 2 * m, 8:72, :] + buf[f, 13 + 2 * m, 8:72, :]
                )
                summed = half[0, pl.ds(0, 32, stride=2), :] + half[0, pl.ds(1, 32, stride=2), :]
                at = 32 * (2 * i + m // 2)
                pairs[m % 2, at : at + 32, :] = summed
        packed = jnp.dot(pairs[0, :, :], even_pick, precision=HI, preferred_element_type=F32) + jnp.dot(
            pairs[1, :, :], odd_pick, precision=HI, preferred_element_type=F32
        )
        for i in range(6):
            for dd in range(2):
                send_lift[kind, dd, i, :, :] = packed[32 * i + 16 * dd : 32 * i + 16 * dd + 16, :]
        for dd in range(2):
            sid = ID_LIFT + 2 * kind
            send(send_lift.at[kind, dd], got_lift.at[kind, par], sid + dd, sid + par, owners[dd], true, True)

    def settle(kind, buf, fields):
        for h in range(2):
            receive(got_lift.at[kind, h], ID_LIFT + 2 * kind + h)
        for i, f in enumerate(fields):
            for mm in range(2):
                e_pack = got_lift[kind, 0, 2 * i + mm, :, :]
                o_pack = got_lift[kind, 1, 2 * i + mm, :, :]
                buf[f, 2 * mm, 8:24, :] = jnp.where(low, e_pack, shifted(o_pack, 64))
                buf[f, 2 * mm + 1, 8:24, :] = jnp.where(low, shifted(e_pack, 64), o_pack)

    for i in (6, 7, 8):
        loads[i].wait()
    lift(0, vb, (0, 1, 2))

    fine_receive(3, 1, vb, VX, VYSIGN)
    stress_update(vb, sb, mb, corr, 8, 8, 64)
    lift(1, sb, (2, 4, 5))
    emit(sb.at[:, 12:20, 8:72, :], fout.at[3:9, 8:16])
    fine_receive(3, 0, vb, VX, VYSIGN)
    stress_update(vb, sb, mb, corr, 0, 8, 64)
    emit(sb.at[:, 4:12, 8:72, :], fout.at[3:9, 0:8])

    loads[9].wait()
    settle(0, cvb, (0, 1, 2))
    settle(1, csb, (2, 4, 5))
    velocity_update(cvb, csb, cmb, ccorr, 0, 8, 16)
    coarse_send(1, cvb, VX, VY)
    emit(cvb.at[:, 4:12, 8:24, :], cout.at[0:3])
    coarse_receive(1, cvb, VX, VYSIGN)
    stress_update(cvb, csb, cmb, ccorr, 0, 8, 16)
    emit(csb.at[:, 4:12, 8:24, :], cout.at[3:9])

    for copy in outs:
        copy.wait()
    for cond, copy in sent:

        @pl.when(cond)
        def _(copy=copy):
            copy().wait_send()


def solution(mesh):
    nx, ny = mesh.shape["gx"], mesh.shape["gy"]

    def body(fs, fm, cs, cm, cp, prow, pcol):
        any_spec = pl.BlockSpec(memory_space=pl.ANY)

        def v(*shape):
            return pltpu.VMEM(shape, F32)

        def call(*refs):
            kernel(nx, ny, *refs)

        return pl.pallas_call(
            call,
            out_shape=(jax.ShapeDtypeStruct(fs.shape, F32), jax.ShapeDtypeStruct(cs.shape, F32)),
            in_specs=[any_spec] * 5
            + [pl.BlockSpec(memory_space=pltpu.SMEM), pl.BlockSpec(memory_space=pltpu.VMEM)],
            out_specs=(any_spec, any_spec),
            scratch_shapes=[
                v(3, 24, 80, 128), v(6, 24, 80, 128), v(3, 16, 64, 128), v(6, 8, 64, 128),
                v(8, 2, 3, 4, 8, 128), v(8, 2, 3, 4, 8, 128), v(8, 2, 64, 128), v(8, 2, 64, 128), v(2, 64, 128),
                v(3, 16, 32, 128), v(6, 16, 32, 128), v(3, 8, 16, 128), v(9, 2, 16, 128),
                v(2, 2, 3, 4, 8, 128), v(2, 2, 3, 4, 8, 128), v(2, 2, 16, 128), v(2, 2, 16, 128), v(2, 16, 128),
                v(2, 13, 16, 128), v(2, 16, 128), v(2, 16, 128), v(2, 8, 128),
                v(2, 13, 16, 128), v(2, 16, 128), v(2, 16, 128), v(2, 8, 128),
                v(14, 40, 128), v(14, 64, 128), v(24, 64, 128), v(2, 64, 128), v(2, 192, 128),
                v(2, 2, 6, 16, 128), v(2, 2, 6, 16, 128),
                pltpu.SemaphoreType.DMA((N_MSG,)), pltpu.SemaphoreType.DMA((N_MSG,)),
                pltpu.SemaphoreType.DMA((10,)), pltpu.SemaphoreType.DMA((8,)),
            ],
            compiler_params=pltpu.CompilerParams(collective_id=0, has_side_effects=True),
            name="slabs",
        )(fs, fm, cs, cm, cp, prow, pcol)

    return jax.shard_map(
        body,
        mesh=mesh,
        in_specs=(
            P(None, None, "gx", "gy"),
            P(None, None, "gx", "gy"),
            P(None, None, "gy", "gx"),
            P(None, None, "gy", "gx"),
            P(None, None, "gy", "gx"),
            P("gx"),
            P("gy"),
        ),
        out_specs=(P(None, None, "gx", "gy"), P(None, None, "gy", "gx")),
        check_vma=False,
    )
```

time: 687 us -> 89.5 us (0.13); the launches traced: 675 us -> 89.4 us
  other arithmetic: 256 us -> 0 us
  local copies, waits for them, and re-layouts: 222 us -> 6.12 us
  starting transfers between devices: 134 us -> 0 us
  Pallas kernels: 0 us -> 82.6 us
  waiting for transfers between devices: 49.3 us -> 0 us
  blocking collectives: 11.7 us -> 0 us
    ppermute x28 -> x0, starting transfers between devices: 82.8 us -> none  [the longest x14 52.4 us: extended(): after = lax.ppermute(leading, axis, down)]
    pallas_call x0 -> x1, Pallas kernels: none -> 82.6 us  [body(): pl.pallas_call(call, out_shape=(jax.ShapeDtypeStruct(fs.shape, F32), jax....]
    unnamed x154 -> x4, local copies, waits for them, and re-layouts: 69.5 us -> 6.12 us
    concatenate x13 -> x0, other arithmetic: 61.2 us -> none  [the longest x4 35.9 us: below_pad(): jnp.concatenate([zero_layers(widened, 4), widened, widen_ghost(widened, g...]
    another operation x12 -> x0, other arithmetic: 57.5 us -> none  [the longest x9 46.2 us: velocity_step(): jnp.stack([first_rate, second_rate, third_rate])]
    slice x34 -> x0, local copies, waits for them, and re-layouts: 56.1 us -> none  [the longest x11 27.7 us: extended(): last = lax.slice_in_dim(x, length - width, length, axis=dim)]
    all_to_all x8 -> x0, starting transfers between devices: 50.8 us -> none  [the longest x3 17.9 us: regrid(): lax.all_to_all(moved_pair, 'gx', split_axis=1, concat_axis=4, tiled=True)]
    ppermute x28 -> x0, waiting for transfers between devices: 44 us -> none  [the longest x14 33.7 us: extended(): before = lax.ppermute(last, axis, up)]
  transfers between devices with their start and end apart: 36 -> 0, of which waited for: 16 -> 0; matrix products, arithmetic and copies ran while one was open for 21% -> 0% of each run, Pallas kernels for 0% -> 0%
where the time goes in v1:
time: 89.5 us; the launch traced here: 89.4 us
  Pallas kernels  82.6 us (92%)
  local copies, waits for them, and re-layouts  6.12 us (7%)
    pallas_call x1, Pallas kernels, body(): pl.pallas_call(call, out_shape=(jax.ShapeDtypeStruct(fs.shape, F32), jax....  82.6 us
    unnamed x4, local copies, waits for them, and re-layouts  6.12 us

profile of v1, /device:TPU:28, one launch (start us, length us, event | category | flops | bytes accessed | tf_op | source)
XLA Modules:
  0.0 89.4 jit_solution(5912620997449754412)
XLA Ops:
  0.6 82.6 %slabs.1 = (f32[9,16,64,128]{3,2,1,0:T(8,128)}, f32[9,8,16,128]{3,2,1,0:T(8,128)}) custom-call(f32[9,16,64,128]{3,2,1,0:T(8,128)} %refs_0_.1, f32[3,16,64,128]{3,2,1,0:T(8,128)} %refs_1_.1, f32[9,8,16,128]{3,2,1,0:T(8,128)} %refs_2_.1, f32[3,8,16,128]{3,2,1,0:T(8,128)} %refs_3_.1, f32[9,2,16,128]{3,2,1,0:T(8,128)} %refs_4_.1, s32[64]{0:T(128)} %refs_5_.1, ...), custom_call_target="tpu_custom_call" | custom-call | tf_op jit(solution)/shard_map/slabs/pallas_call | solution.py:610
  83.3 0.0 copy-start
  83.3 5.3 %copy.11 = f32[9,16,64,128]{3,2,1,0:T(8,128)} copy(f32[9,16,64,128]{3,2,1,0:T(8,128)} %get-tuple-element.4) | data formatting | bytes 9437184
  88.6 0.0 copy-done
  88.6 0.8 copy.12
Async XLA Ops:
  83.3 5.3 %copy-start = (f32[9,8,16,128]{3,2,1,0:T(8,128)S(1)}, f32[9,8,16,128]{3,2,1,0:T(8,128)}, u32[]{:S(2)}) copy-start(f32[9,8,16,128]{3,2,1,0:T(8,128)} %get-tuple-element.5) | copy-start | bytes 1769476
